TPU v7x, 128 devices: a whole 4x4x4 slice. The times are simulated.
128 devices in a mesh: seq: 32 (over y, z, core), head: 4 (over x).
Axes of the slice: x: 4, y: 4, z: 4, core: 2. Of those that a mesh axis runs over, the one named last changes fastest.
Arguments:
- vision: bfloat16 [65536, 7680], P(('seq', 'head')), may hold values from -6 to 6
- w_key: bfloat16 [7680, 512], replicated, may hold values from -0.0625 to 0.0625
- w_value: bfloat16 [7680, 512], replicated, may hold values from -0.0625 to 0.0625
- queries: bfloat16 [256, 4096], P('seq', 'head'), may hold values from -240 to 240
- w_out: bfloat16 [4096, 8192], P('head', 'seq'), may hold values from -0.09375 to 0.09375
Outputs:
- mixed: bfloat16 [256, 8192], P('head', 'seq')
All inputs are finite; a program needn't handle non-finite values.
Results may differ from a plain program's by a relative error of at most 0.03.
Values may be sent and summed in bfloat16 or wider, within the bound.
No kernel may reach another device: no remote copies, remote signals or barrier semaphores. Data moves between devices by JAX's collectives and lax.ppermute only.
A program may use at most 128 MiB of HBM per device.

v0:
```python
import jax
import jax.numpy as jnp
from jax import lax
from jax.sharding import PartitionSpec as P

HD = 128


def scale_rows(partial_value, factor):
    return (
        partial_value.reshape(factor.shape[0], factor.shape[1], -1) * factor[:, :, None]
    ).reshape(factor.shape[0], -1)


def divide_rows(partial_value, denom):
    return (partial_value.reshape(denom.shape[0], denom.shape[1], -1) / denom[:, :, None]).reshape(
        denom.shape[0], -1
    )


def attend(queries_all, keys_here, values_here):
    head_size = HD
    kv_local = keys_here.shape[1] // head_size
    text_rows = queries_all.shape[0]
    q_heads = queries_all.shape[1] // head_size
    group_size = q_heads // kv_local
    grouped = queries_all.reshape(text_rows, kv_local, group_size, head_size)
    key_heads = keys_here.reshape(keys_here.shape[0], kv_local, head_size)
    value_heads = values_here.reshape(values_here.shape[0], kv_local, head_size)
    scores = jnp.einsum(
        "tkgd,nkd->kgtn", grouped, key_heads, preferred_element_type=jnp.float32
    ) * head_size ** (-0.5)
    maxima = jnp.max(scores, axis=-1)
    powers = jnp.exp(scores - maxima[..., None])
    totals = jnp.sum(powers, axis=-1)
    partial_value = jnp.einsum(
        "kgtn,nkd->tkgd",
        powers.astype(jnp.bfloat16),
        value_heads,
        preferred_element_type=jnp.float32,
    )
    partial_value = partial_value.reshape(text_rows, q_heads * head_size)
    maxima = maxima.transpose(2, 0, 1).reshape(text_rows, q_heads)
    totals = totals.transpose(2, 0, 1).reshape(text_rows, q_heads)
    return (maxima, totals, partial_value)


def shards(vision, w_key, w_value, queries, w_out):
    keys = jnp.dot(vision, w_key, preferred_element_type=jnp.float32).astype(jnp.bfloat16)
    values = jnp.dot(vision, w_value, preferred_element_type=jnp.float32).astype(jnp.bfloat16)
    keys_here, values_here = (
        lax.all_to_all(keys, "head", split_axis=1, concat_axis=0, tiled=True),
        lax.all_to_all(values, "head", split_axis=1, concat_axis=0, tiled=True),
    )
    queries_all = lax.all_gather(queries, "seq", axis=0, tiled=True)
    maxima, totals, partial_value = attend(queries_all, keys_here, values_here)
    global_max = lax.pmax(maxima, "seq")
    factor = jnp.exp(maxima - global_max)
    denom, numer = (
        lax.psum((totals * factor).astype(jnp.bfloat16), "seq").astype(jnp.float32),
        lax.psum(scale_rows(partial_value, factor).astype(jnp.bfloat16), "seq").astype(jnp.float32),
    )
    attended = divide_rows(numer, denom).astype(jnp.bfloat16)
    return lax.psum_scatter(
        jnp.dot(attended, w_out, preferred_element_type=jnp.float32).astype(jnp.bfloat16),
        "head",
        scatter_dimension=0,
        tiled=True,
    )


def solution(mesh):
    placed = (P(("seq", "head"), None), P(), P(), P("seq", "head"), P("head", "seq"))
    return jax.shard_map(
        shards, mesh=mesh, in_specs=placed, out_specs=P("head", "seq"), check_vma=False
    )
```

profile of v0, /device:TPU:0, one launch (start us, length us, event | category | flops | bytes accessed | tf_op | source)
XLA Modules:
  0.0 286.8 jit_solution(6718358822578115209)
XLA Ops:
  6.5 10.6 %convolution_convert_fusion.1 = bf16[512,512]{0,1:T(8,128)(2,1)} fusion(bf16[512,7680]{1,0:T(8,128)(2,1)} %param.5, bf16[7680,512]{1,0:T(8,128)(2,1)} %param.7), kind=kOutput, calls=%fused_computation.8 | convolution fusion | flops 4026793984 | bytes 16252928 | tf_op jit(solution)/shard_map/dot_general | solution.py:50
  17.1 4.5 %all-to-all-start = ((bf16[512,4,128]{0,2,1:T(8,128)(2,1)}), bf16[512,4,128]{0,2,1:T(8,128)(2,1)S(1)}, u32[]{:S(2)}, u32[]{:S(2)}) async-start(bf16[512,4,128]{0,2,1:T(8,128)(2,1)} %bitcast), calls=%async_computation | async-start | bytes 1048576 | tf_op jit(solution)/shard_map/all_to_all | solution.py:53
  21.7 10.5 %convolution_convert_fusion = bf16[512,512]{0,1:T(8,128)(2,1)} fusion(bf16[512,7680]{1,0:T(8,128)(2,1)} %param.5, bf16[7680,512]{1,0:T(8,128)(2,1)} %param.6), kind=kOutput, calls=%fused_computation.7 | convolution fusion | flops 4026793984 | bytes 16252928 | tf_op jit(solution)/shard_map/dot_general | solution.py:49
  32.2 0.0 all-to-all-done
  32.2 4.8 %all-to-all-start.1 = ((bf16[512,4,128]{0,2,1:T(8,128)(2,1)}), bf16[512,4,128]{0,2,1:T(8,128)(2,1)S(1)}, u32[]{:S(2)}, u32[]{:S(2)}) async-start(bf16[512,4,128]{0,2,1:T(8,128)(2,1)} %bitcast.2), calls=%async_computation.1 | async-start | bytes 1048576 | tf_op jit(solution)/shard_map/all_to_all | solution.py:52
  37.0 26.5 %all_gather.3 = bf16[256,1024]{1,0:T(8,128)(2,1)S(1)} all-gather(bf16[8,1024]{1,0:T(8,128)(2,1)S(1)} %copy-done.1), channel_id=1, replica_groups=mesh['seq'=32,'head'=4] {'seq'}, dimensions={0}, use_global_device_ids=true | all-gather | bytes 540672 | tf_op jit(solution)/shard_map/all_gather | solution.py:55
  63.5 0.2 copy.16
  63.7 0.4 copy.14
  64.1 0.4 reshape.57
  64.5 0.0 all-to-all-done.1
  64.5 0.3 copy.15
  64.8 8.0 %bitcast_reduce_fusion = (f32[8,256]{1,0:T(8,128)S(1)}, f32[2048,256,8]{1,0,2:T(8,128)}) fusion(bf16[2048,128,1]{1,0,2:T(8,128)(2,1)S(1)} %bitcast.66, bf16[256,8,128]{0,2,1:T(8,128)(2,1)S(1)} %bitcast.65), kind=kOutput, calls=%fused_computation.1 | convolution fusion | flops 1082128384 | bytes 17833984 | tf_op jit(solution)/shard_map/tkgd,nkd->kgtn/dot_general | solution.py:30
  72.8 8.5 %fusion.1 = f32[8,256]{1,0:T(8,128)S(1)} fusion(f32[2048,256,8]{1,0,2:T(8,128)} %get-tuple-element.8, f32[8,256]{1,0:T(8,128)S(1)} %get-tuple-element.7), kind=kLoop, calls=%fused_computation.3 | loop fusion | flops 12580864 | bytes 16793600 | tf_op jit(solution)/shard_map/reduce_sum | solution.py:35
  81.3 7.4 %fusion.4 = f32[128,8,256]{2,0,1:T(8,128)S(1)} fusion(bf16[2048,128,1]{0,1,2:T(8,128)(2,1)S(1)} %reshape.57, f32[2048,256,8]{1,0,2:T(8,128)} %get-tuple-element.8, f32[8,256]{1,0:T(8,128)S(1)} %get-tuple-element.7), kind=kOutput, calls=%fused_computation.6 | convolution fusion | flops 1086324736 | bytes 18358272 | tf_op jit(solution)/shard_map/kgtn,nkd->tkgd/dot_general | solution.py:36
  88.7 66.3 %pmax.7 = f32[256,8]{0,1:T(8,128)S(1)} all-reduce(f32[256,8]{0,1:T(8,128)S(1)} %bitcast.69), channel_id=1, replica_groups=mesh['seq'=32,'head'=4] {'seq'}, use_global_device_ids=true, to_apply=%region_1.0 | all-reduce | flops 2048 | bytes 16384 | tf_op jit(solution)/shard_map/pmax | solution.py:57
  155.1 0.9 fusion.6
  156.0 0.0 all-reduce.2.cloned.1.call-update
  156.0 0.0 reduce-scatter.2.cloned.1.call-start
  156.0 62.8 %psum.15 = bf16[256,8]{0,1:T(8,128)(2,1)S(1)} all-reduce(bf16[256,8]{0,1:T(8,128)(2,1)S(1)} %get-tuple-element.5), channel_id=1, replica_groups=mesh['seq'=32,'head'=4] {'seq'}, use_global_device_ids=true, to_apply=%region_4.0 | all-reduce | flops 2048 | bytes 8192 | tf_op jit(solution)/shard_map/psum | solution.py:60
  218.8 38.6 %all-reduce.2.cloned.1.call-done = bf16[256,1024]{0,1:T(8,128)(2,1)} async-done(((bf16[256,1024]{0,1:T(8,128)(2,1)}), bf16[256,1024]{0,1:T(8,128)(2,1)}) %all-reduce.2.cloned.1.call-update) | async-done | bytes 524304 | tf_op jit(solution)/shard_map/psum | solution.py:61
  257.4 1.1 fusion.7
  258.6 1.0 convolution_convert_fusion.2
  259.6 0.0 reduce-scatter.2.cloned.1.call-update
  259.6 20.4 %reduce-scatter.2.cloned.1.call-done = bf16[64,256]{1,0:T(8,128)(2,1)} async-done(((bf16[256,256]{1,0:T(8,128)(2,1)}), bf16[64,256]{1,0:T(8,128)(2,1)}) %reduce-scatter.2.cloned.1.call-update) | async-done | bytes 32784 | tf_op jit(solution)/shard_map/reduce_scatter | solution.py:64
  (7 shorter events, 0.0 us)
Async XLA Ops:
  6.5 252.0 %copy-start = (bf16[1024,256]{1,0:T(8,128)(2,1)S(1)}, bf16[1024,256]{1,0:T(8,128)(2,1)}, u32[]{:S(2)}) copy-start(bf16[1024,256]{1,0:T(8,128)(2,1)} %param.9) | copy-start | bytes 1572868
  17.1 19.9 %copy-start.1 = (bf16[8,1024]{1,0:T(8,128)(2,1)S(1)}, bf16[8,1024]{1,0:T(8,128)(2,1)}, u32[]{:S(2)}) copy-start(bf16[8,1024]{1,0:T(8,128)(2,1)} %param.8) | copy-start | bytes 49156
  17.1 15.1 %all-to-all-start = ((bf16[512,4,128]{0,2,1:T(8,128)(2,1)}), bf16[512,4,128]{0,2,1:T(8,128)(2,1)S(1)}, u32[]{:S(2)}, u32[]{:S(2)}) async-start(bf16[512,4,128]{0,2,1:T(8,128)(2,1)} %bitcast), calls=%async_computation | async-start | bytes 1048576 | tf_op jit(solution)/shard_map/all_to_all | solution.py:53
  32.2 32.3 %all-to-all-start.1 = ((bf16[512,4,128]{0,2,1:T(8,128)(2,1)}), bf16[512,4,128]{0,2,1:T(8,128)(2,1)S(1)}, u32[]{:S(2)}, u32[]{:S(2)}) async-start(bf16[512,4,128]{0,2,1:T(8,128)(2,1)} %bitcast.2), calls=%async_computation.1 | async-start | bytes 1048576 | tf_op jit(solution)/shard_map/all_to_all | solution.py:52
  37.0 220.4 %all-reduce.2.cloned.1.call-start = ((), (), s32[]{:S(2)}) async-start(), calls=%async_computation.3 | async-start | bytes 1048576 | tf_op jit(solution)/shard_map/psum | solution.py:61
  156.0 124.0 %reduce-scatter.2.cloned.1.call-start = ((), (), s32[]{:S(2)}) async-start(), calls=%async_computation.4 | async-start | bytes 163840 | tf_op jit(solution)/shard_map/reduce_scatter | solution.py:64
Sparse Core Ops, SparseCore 0:
  156.1 101.2 all-reduce.1
  259.8 20.1 reduce-scatter.1
where the time goes:
time: 287 us
  blocking collectives  156 us (54%)
  waiting for transfers between devices  59 us (21%)
  matrix products  37.6 us (13%)
  between operations  13.5 us (5%)
  other arithmetic  10.5 us (4%)
  starting transfers between devices  9.38 us (3%)
    pmax x1, blocking collectives, shards(): global_max = lax.pmax(maxima, 'seq')  66.3 us
    psum x1, blocking collectives, shards(): lax.psum((totals * factor).astype(jnp.bfloat16), 'seq').astype(jnp.float32)  62.8 us
    psum x1, waiting for transfers between devices, shards(): lax.psum(scale_rows(partial_value, factor).astype(jnp.bfloat16), 'seq')  38.6 us
    all_gather x1, blocking collectives, shards(): queries_all = lax.all_gather(queries, 'seq', axis=0, tiled=True)  26.5 us
    reduce_scatter x1, waiting for transfers between devices, shards(): lax.psum_scatter(jnp.dot(attended, w_out, preferred_element_type=jnp.floa...  20.4 us
    dot_general x1, matrix products, shards(): jnp.dot(vision, w_value, preferred_element_type=jnp.float32)  10.6 us
    dot_general x1, matrix products, shards(): jnp.dot(vision, w_key, preferred_element_type=jnp.float32)  10.5 us
    reduce_sum x1, other arithmetic, attend(): totals = jnp.sum(powers, axis=-1)  8.48 us
  transfers between devices with their start and end apart: 4, of which 2 were waited for; matrix products, arithmetic and copies ran while one was open for 4% of the time, Pallas kernels for 0%

commit v1 on v0

--- a/solution.py
+++ b/solution.py
@@ -4,6 +4,10 @@
 from jax.sharding import PartitionSpec as P
 
 HD = 128
+
+
+def drive_the_edge(inner_x):
+    return jnp.sum(lax.all_gather(inner_x, axis_name="seq"), 0)
 
 
 def scale_rows(partial_value, factor):
@@ -57,7 +61,7 @@
     global_max = lax.pmax(maxima, "seq")
     factor = jnp.exp(maxima - global_max)
     denom, numer = (
-        lax.psum((totals * factor).astype(jnp.bfloat16), "seq").astype(jnp.float32),
+        drive_the_edge((totals * factor).astype(jnp.bfloat16)).astype(jnp.float32),
         lax.psum(scale_rows(partial_value, factor).astype(jnp.bfloat16), "seq").astype(jnp.float32),
     )
     attended = divide_rows(numer, denom).astype(jnp.bfloat16)

time: 287 us -> 288 us (level)
  blocking collectives: 156 us -> 114 us
  waiting for transfers between devices: 59 us -> 101 us
    psum x1 -> x0, blocking collectives: 62.8 us -> none  [shards(): lax.psum((totals * factor).astype(jnp.bfloat16), 'seq').astype(jnp.float32)]
    psum x1, waiting for transfers between devices: 38.6 us -> 80.7 us  [shards(): lax.psum(scale_rows(partial_value, factor).astype(jnp.bfloat16), 'seq')]
    all_gather x0 -> x1, blocking collectives: none -> 21.1 us  [drive_the_edge(): return jnp.sum(lax.all_gather(inner_x, axis_name='seq'), 0)]
where the time goes in v1:
time: 288 us; the launch traced here: 287 us
  blocking collectives  114 us (40%)
  waiting for transfers between devices  101 us (35%)
  matrix products  37.6 us (13%)
  between operations  13.5 us (5%)
  other arithmetic  10.6 us (4%)
  starting transfers between devices  9.38 us (3%)
    psum x1, waiting for transfers between devices, shards(): lax.psum(scale_rows(partial_value, factor).astype(jnp.bfloat16), 'seq')  80.7 us
    pmax x1, blocking collectives, shards(): global_max = lax.pmax(maxima, 'seq')  66.3 us
    all_gather x1, blocking collectives, shards(): queries_all = lax.all_gather(queries, 'seq', axis=0, tiled=True)  26.5 us
    all_gather x1, blocking collectives, drive_the_edge(): return jnp.sum(lax.all_gather(inner_x, axis_name='seq'), 0)  21.1 us
    reduce_scatter x1, waiting for transfers between devices, shards(): lax.psum_scatter(jnp.dot(attended, w_out, preferred_element_type=jnp.floa...  20.4 us
    dot_general x1, matrix products, shards(): jnp.dot(vision, w_value, preferred_element_type=jnp.float32)  10.6 us
    dot_general x1, matrix products, shards(): jnp.dot(vision, w_key, preferred_element_type=jnp.float32)  10.5 us
    reduce_sum x1, other arithmetic, attend(): totals = jnp.sum(powers, axis=-1)  8.48 us
  transfers between devices with their start and end apart: 4, of which 2 were waited for; matrix products, arithmetic and copies ran while one was open for 4% of the time, Pallas kernels for 0%

profile of v1, /device:TPU:0, one launch (start us, length us, event | category | flops | bytes accessed | tf_op | source)
XLA Modules:
  0.0 287.3 jit_solution(17784836179455780720)
XLA Ops:
  6.5 10.6 %convolution_convert_fusion.1 = bf16[512,512]{0,1:T(8,128)(2,1)} fusion(bf16[512,7680]{1,0:T(8,128)(2,1)} %param.5, bf16[7680,512]{1,0:T(8,128)(2,1)} %param.7), kind=kOutput, calls=%fused_computation.8 | convolution fusion | flops 4026793984 | bytes 16252928 | tf_op jit(solution)/shard_map/dot_general | solution.py:54
  17.1 4.5 %all-to-all-start = ((bf16[512,4,128]{0,2,1:T(8,128)(2,1)}), bf16[512,4,128]{0,2,1:T(8,128)(2,1)S(1)}, u32[]{:S(2)}, u32[]{:S(2)}) async-start(bf16[512,4,128]{0,2,1:T(8,128)(2,1)} %bitcast), calls=%async_computation | async-start | bytes 1048576 | tf_op jit(solution)/shard_map/all_to_all | solution.py:57
  21.7 10.5 %convolution_convert_fusion = bf16[512,512]{0,1:T(8,128)(2,1)} fusion(bf16[512,7680]{1,0:T(8,128)(2,1)} %param.5, bf16[7680,512]{1,0:T(8,128)(2,1)} %param.6), kind=kOutput, calls=%fused_computation.7 | convolution fusion | flops 4026793984 | bytes 16252928 | tf_op jit(solution)/shard_map/dot_general | solution.py:53
  32.2 0.0 all-to-all-done
  32.2 4.8 %all-to-all-start.1 = ((bf16[512,4,128]{0,2,1:T(8,128)(2,1)}), bf16[512,4,128]{0,2,1:T(8,128)(2,1)S(1)}, u32[]{:S(2)}, u32[]{:S(2)}) async-start(bf16[512,4,128]{0,2,1:T(8,128)(2,1)} %bitcast.2), calls=%async_computation.1 | async-start | bytes 1048576 | tf_op jit(solution)/shard_map/all_to_all | solution.py:56
  37.0 26.5 %all_gather.9 = bf16[256,1024]{1,0:T(8,128)(2,1)S(1)} all-gather(bf16[8,1024]{1,0:T(8,128)(2,1)S(1)} %copy-done.1), channel_id=1, replica_groups=mesh['seq'=32,'head'=4] {'seq'}, dimensions={0}, use_global_device_ids=true | all-gather | bytes 540672 | tf_op jit(solution)/shard_map/all_gather | solution.py:59
  63.5 0.2 copy.16
  63.7 0.4 copy.14
  64.1 0.4 reshape.60
  64.5 0.0 all-to-all-done.1
  64.5 0.3 copy.15
  64.8 8.0 %bitcast_reduce_fusion = (f32[8,256]{1,0:T(8,128)S(1)}, f32[2048,256,8]{1,0,2:T(8,128)}) fusion(bf16[2048,128,1]{1,0,2:T(8,128)(2,1)S(1)} %bitcast.67, bf16[256,8,128]{0,2,1:T(8,128)(2,1)S(1)} %bitcast.66), kind=kOutput, calls=%fused_computation.1 | convolution fusion | flops 1082128384 | bytes 17833984 | tf_op jit(solution)/shard_map/tkgd,nkd->kgtn/dot_general | solution.py:34
  72.8 8.5 %fusion.1 = f32[8,256]{1,0:T(8,128)S(1)} fusion(f32[2048,256,8]{1,0,2:T(8,128)} %get-tuple-element.8, f32[8,256]{1,0:T(8,128)S(1)} %get-tuple-element.7), kind=kLoop, calls=%fused_computation.3 | loop fusion | flops 12580864 | bytes 16793600 | tf_op jit(solution)/shard_map/reduce_sum | solution.py:39
  81.3 7.4 %fusion.4 = f32[128,8,256]{2,0,1:T(8,128)S(1)} fusion(bf16[2048,128,1]{0,1,2:T(8,128)(2,1)S(1)} %reshape.60, f32[2048,256,8]{1,0,2:T(8,128)} %get-tuple-element.8, f32[8,256]{1,0:T(8,128)S(1)} %get-tuple-element.7), kind=kOutput, calls=%fused_computation.6 | convolution fusion | flops 1086324736 | bytes 18358272 | tf_op jit(solution)/shard_map/kgtn,nkd->tkgd/dot_general | solution.py:40
  88.7 66.3 %pmax.7 = f32[256,8]{0,1:T(8,128)S(1)} all-reduce(f32[256,8]{0,1:T(8,128)S(1)} %bitcast.71), channel_id=1, replica_groups=mesh['seq'=32,'head'=4] {'seq'}, use_global_device_ids=true, to_apply=%region_1.0 | all-reduce | flops 2048 | bytes 16384 | tf_op jit(solution)/shard_map/pmax | solution.py:61
  155.1 0.9 fusion.6
  156.0 0.0 all-reduce.2.cloned.1.call-update
  156.0 0.0 reduce-scatter.2.cloned.1.call-start
  156.0 21.1 %all-gather = bf16[8192,8]{0,1:T(8,128)(2,1)S(1)} all-gather(bf16[256,8]{0,1:T(8,128)(2,1)S(1)} %get-tuple-element.5), channel_id=2, replica_groups=mesh['seq'=32,'head'=4] {'seq'}, dimensions={0}, use_global_device_ids=true | all-gather | bytes 135168 | tf_op jit(solution)/shard_map/all_gather | solution.py:10
  177.2 80.7 %all-reduce.2.cloned.1.call-done = bf16[256,1024]{0,1:T(8,128)(2,1)} async-done(((bf16[256,1024]{0,1:T(8,128)(2,1)}), bf16[256,1024]{0,1:T(8,128)(2,1)}) %all-reduce.2.cloned.1.call-update) | async-done | bytes 524304 | tf_op jit(solution)/shard_map/psum | solution.py:65
  257.9 1.1 fusion.7
  259.0 1.0 convolution_convert_fusion.2
  260.0 0.0 reduce-scatter.2.cloned.1.call-update
  260.0 20.4 %reduce-scatter.2.cloned.1.call-done = bf16[64,256]{1,0:T(8,128)(2,1)} async-done(((bf16[256,256]{1,0:T(8,128)(2,1)}), bf16[64,256]{1,0:T(8,128)(2,1)}) %reduce-scatter.2.cloned.1.call-update) | async-done | bytes 32784 | tf_op jit(solution)/shard_map/reduce_scatter | solution.py:68
  (8 shorter events, 0.1 us)
Async XLA Ops:
  6.5 252.5 %copy-start = (bf16[1024,256]{1,0:T(8,128)(2,1)S(1)}, bf16[1024,256]{1,0:T(8,128)(2,1)}, u32[]{:S(2)}) copy-start(bf16[1024,256]{1,0:T(8,128)(2,1)} %param.9) | copy-start | bytes 1572868
  17.1 19.9 %copy-start.1 = (bf16[8,1024]{1,0:T(8,128)(2,1)S(1)}, bf16[8,1024]{1,0:T(8,128)(2,1)}, u32[]{:S(2)}) copy-start(bf16[8,1024]{1,0:T(8,128)(2,1)} %param.8) | copy-start | bytes 49156
  17.1 15.1 %all-to-all-start = ((bf16[512,4,128]{0,2,1:T(8,128)(2,1)}), bf16[512,4,128]{0,2,1:T(8,128)(2,1)S(1)}, u32[]{:S(2)}, u32[]{:S(2)}) async-start(bf16[512,4,128]{0,2,1:T(8,128)(2,1)} %bitcast), calls=%async_computation | async-start | bytes 1048576 | tf_op jit(solution)/shard_map/all_to_all | solution.py:57
  32.2 32.3 %all-to-all-start.1 = ((bf16[512,4,128]{0,2,1:T(8,128)(2,1)}), bf16[512,4,128]{0,2,1:T(8,128)(2,1)S(1)}, u32[]{:S(2)}, u32[]{:S(2)}) async-start(bf16[512,4,128]{0,2,1:T(8,128)(2,1)} %bitcast.2), calls=%async_computation.1 | async-start | bytes 1048576 | tf_op jit(solution)/shard_map/all_to_all | solution.py:56
  37.0 220.9 %all-reduce.2.cloned.1.call-start = ((), (), s32[]{:S(2)}) async-start(), calls=%async_computation.3 | async-start | bytes 1048576 | tf_op jit(solution)/shard_map/psum | solution.py:65
  156.0 124.4 %reduce-scatter.2.cloned.1.call-start = ((), (), s32[]{:S(2)}) async-start(), calls=%async_computation.4 | async-start | bytes 163840 | tf_op jit(solution)/shard_map/reduce_scatter | solution.py:68
Sparse Core Ops, SparseCore 0:
  156.1 101.7 all-reduce.1
  260.2 20.1 reduce-scatter.1
